TPU v7x, 32 devices: a whole 2x2x4 slice. The times are simulated.
32 devices in a mesh: op: 8 (over y, x, core), tm: 4 (over z).
Axes of the slice: x: 2, y: 2, z: 4, core: 2. Of those that a mesh axis runs over, the one named last changes fastest.
Arguments:
- phi: bfloat16 [256, 32, 2, 128, 128], P('op', 'tm'), may hold values from -6 to 6
- tau_fwd: bfloat16 [2, 32, 2, 128, 128], P(None, 'tm'), may hold values from -0.375 to 0.375
- tau_bwd: bfloat16 [2, 32, 2, 128, 128], P(None, 'tm'), may hold values from -0.375 to 0.375
- src_times: int32 [2], replicated, may hold values from 0 to 31
- partner: int32 [256], replicated, may hold values from 0 to 255, each once
Outputs:
- corr: float32 [256, 2, 32, 2, 256], P('op', None, 'tm')
Inputs may be any that keep to these rules, and one draw needn't show every extreme that they name: partner is a permutation of the operators. `src_times`: source times may repeat.
All inputs are finite; a program needn't handle non-finite values.
Results may differ from a plain program's by a relative error of at most 0.0041.
Values may be sent and summed in bfloat16 or wider, within the bound.
A program may use at most 256 MiB of HBM per device.

v0:
```python
import jax
import jax.numpy as jnp
from jax import lax
from jax.sharding import PartitionSpec as P


def from_root(value, axis, source):
    kept = jnp.where(lax.axis_index(axis) == source, value, 0).astype(value.dtype)
    return lax.psum(kept, axis)


def complex_product(spec, left_re, left_im, right_re, right_im):

    def inner(first, second):
        return jnp.einsum(spec, first, second, preferred_element_type=jnp.float32)

    return (
        inner(left_re, right_re) - inner(left_im, right_im),
        inner(left_re, right_im) + inner(left_im, right_re),
    )


def corr_block(panel, source):
    width = panel.shape[-1]
    sink_re = panel[:, :, :, 0]
    sink_im = panel[:, :, :, 1]
    source_re = source[:, :, 0]
    source_im = source[:, :, 1]

    def inner(first, second):
        return jnp.einsum("jstad,ksad->jstk", first, second, preferred_element_type=jnp.float32)

    real_part = inner(sink_re, source_re) + inner(sink_im, source_im)
    imag_part = inner(sink_im, source_re) - inner(sink_re, source_im)
    return jnp.stack([real_part, imag_part], 3) / width


def body(phi, tau_fwd, tau_bwd, src_times, partner):
    time_local = phi.shape[1]
    sources = tau_fwd.shape[0]
    left_re, left_im = complex_product(
        "stab,jtbc->jstac", tau_fwd[:, :, 0], tau_fwd[:, :, 1], phi[:, :, 0], phi[:, :, 1]
    )
    left_re = left_re.astype(jnp.bfloat16)
    left_im = left_im.astype(jnp.bfloat16)
    sink_re, sink_im = complex_product(
        "jstac,stcd->jstad", left_re, left_im, tau_bwd[:, :, 0], tau_bwd[:, :, 1]
    )
    panel = jnp.stack([sink_re.astype(jnp.bfloat16), sink_im.astype(jnp.bfloat16)], 3)
    fields = []
    for source_index in range(sources):
        when = src_times[source_index]
        local = lax.dynamic_index_in_dim(phi, when % time_local, 1, False)
        fields.append(from_root(local, "tm", when // time_local))
    own_sources = jnp.stack(fields, 1)
    mixed = corr_block(panel, lax.all_gather(own_sources, "op", axis=0, tiled=True))
    return jnp.take(mixed, partner, axis=4)


def solution(mesh):
    in_specs = (
        P("op", "tm", None, None, None),
        P(None, "tm", None, None, None),
        P(None, "tm", None, None, None),
        P(),
        P(),
    )
    out_specs = P("op", None, "tm", None, None)
    return jax.shard_map(body, mesh=mesh, in_specs=in_specs, out_specs=out_specs, check_vma=False)
```

profile of v0, /device:TPU:0, one launch (start us, length us, event | category | flops | bytes accessed | tf_op | source)
XLA Modules:
  0.0 562.1 jit_solution(6328620957796238682)
XLA Ops:
  6.5 0.0 all-reduce.3.cloned.1.call-start
  6.5 1.3 fusion.62
  13.0 2.7 constant_dynamic-slice_fusion.1
  15.8 4.6 copy_select_fusion
  20.4 0.0 all-reduce.3.cloned.1.call-update
  20.4 0.0 all-gather.2.cloned.1.call-start
  20.5 157.8 %all-reduce.3.cloned.1.call-done = (bf16[32,1,2,128,128]{4,0,3,1,2:T(8,128)(2,1)}, bf16[32,1,2,128,128]{4,0,3,1,2:T(8,128)(2,1)}) async-done(((bf16[32,1,2,128,128]{4,0,3,1,2:T(8,128)(2,1)}, bf16[32,1,2,128,128]{4,0,3,1,2:T(8,128)(2,1)}), (bf16[32,1,2,128,128]{4,0,3,1,2:T(8,128)(2,1)}, bf16[32,1,2,128,128]{4,0,3,1,2:T(8,128)(2,1)})) %all-reduce.3.cloned.1.call-update) | async-done | bytes 4194320 | tf_op jit(solution)/shard_map/psum | solution.py:9
  178.3 4.6 pad_maximum_fusion
  182.9 0.0 all-gather.2.cloned.1.call-update
  182.9 13.8 %fusion.60 = (bf16[32,8,1,128,128]{4,3,2,1,0:T(8,128)(2,1)}, bf16[32,8,1,128,128]{4,3,2,1,0:T(8,128)(2,1)}) fusion(bf16[32,8,2,128,128]{4,3,2,1,0:T(8,128)(2,1)} %param.5), kind=kLoop, calls=%fused_computation.59 | loop fusion | bytes 33554432 | tf_op jit(solution)/shard_map/slice | solution.py:42
  196.7 0.0 copy-start.2
  196.7 0.0 copy-start.1
  196.7 12.1 %copy.63 = bf16[32,8,1,128,128]{3,4,0,1,2:T(8,128)(2,1)} copy(bf16[32,8,1,128,128]{4,3,2,1,0:T(8,128)(2,1)} %get-tuple-element.10) | data formatting | bytes 16777216
  208.9 11.9 %copy.65 = bf16[32,8,1,128,128]{3,4,0,1,2:T(8,128)(2,1)} copy(bf16[32,8,1,128,128]{4,3,2,1,0:T(8,128)(2,1)} %get-tuple-element.9) | data formatting | bytes 16777216
  220.8 0.0 copy-done.2
  220.8 0.6 pad_clamp_fusion
  221.4 0.5 compare_and_fusion
  222.0 0.0 copy-done.1
  222.0 0.1 fusion.61
  222.1 19.0 %fusion.23 = f32[8,32,128,2,128]{4,2,3,1,0:T(8,128)} fusion(bf16[32,8,1,128,128]{3,4,0,1,2:T(8,128)(2,1)} %copy.63, bf16[2,8,1,128,128]{4,3,2,1,0:T(8,128)(2,1)S(1)} %get-tuple-element.12), kind=kOutput, calls=%fused_computation.26 | convolution fusion | flops 2147483648 | bytes 42467328 | tf_op jit(solution)/shard_map/stab,jtbc->jstac/dot_general | solution.py:15
  241.0 21.0 %fusion.25 = f32[8,32,128,2,128]{4,2,3,1,0:T(8,128)} fusion(bf16[32,8,1,128,128]{3,4,0,1,2:T(8,128)(2,1)} %copy.65, bf16[2,8,1,128,128]{4,3,2,1,0:T(8,128)(2,1)S(1)} %get-tuple-element.12), kind=kOutput, calls=%fused_computation.28 | convolution fusion | flops 2147483648 | bytes 42467328 | tf_op jit(solution)/shard_map/stab,jtbc->jstac/dot_general | solution.py:15
  262.0 20.4 %fusion = bf16[32,2,8,128,128]{3,4,1,0,2:T(8,128)(2,1)} fusion(f32[8,32,128,2,128]{4,2,3,1,0:T(8,128)} %fusion.23, bf16[32,8,1,128,128]{3,4,0,1,2:T(8,128)(2,1)} %copy.65, bf16[2,8,1,128,128]{4,3,2,1,0:T(8,128)(2,1)S(1)} %get-tuple-element.11), kind=kOutput, calls=%fused_computation.5 | convolution fusion | flops 2164260864 | bytes 59244544 | tf_op jit(solution)/shard_map/stab,jtbc->jstac/dot_general | solution.py:15
  282.4 0.0 copy-start
  282.4 21.5 %fusion.1 = bf16[32,2,8,128,128]{3,4,1,0,2:T(8,128)(2,1)} fusion(f32[8,32,128,2,128]{4,2,3,1,0:T(8,128)} %fusion.25, bf16[32,8,1,128,128]{3,4,0,1,2:T(8,128)(2,1)} %copy.63, bf16[2,8,1,128,128]{4,3,2,1,0:T(8,128)(2,1)S(1)} %get-tuple-element.11), kind=kOutput, calls=%fused_computation.6 | convolution fusion | flops 2164260864 | bytes 59244544 | tf_op jit(solution)/shard_map/stab,jtbc->jstac/dot_general | solution.py:15
  303.9 0.0 copy-done
  303.9 17.1 %fusion.10 = f32[2,8,32,128,128]{4,3,2,1,0:T(8,128)} fusion(bf16[32,2,8,128,128]{3,4,1,0,2:T(8,128)(2,1)} %fusion, bf16[2,8,2,128,128]{4,3,2,1,0:T(8,128)(2,1)S(1)} %copy-done), kind=kOutput, calls=%fused_computation.17 | convolution fusion | flops 2147483648 | bytes 50855936 | tf_op jit(solution)/shard_map/jstac,stcd->jstad/dot_general | solution.py:15
  320.9 17.1 %fusion.8 = f32[2,8,32,128,128]{4,3,2,1,0:T(8,128)} fusion(bf16[32,2,8,128,128]{3,4,1,0,2:T(8,128)(2,1)} %fusion, bf16[2,8,2,128,128]{4,3,2,1,0:T(8,128)(2,1)S(1)} %copy-done), kind=kOutput, calls=%fused_computation.15 | convolution fusion | flops 2147483648 | bytes 50855936 | tf_op jit(solution)/shard_map/jstac,stcd->jstad/dot_general | solution.py:15
  338.0 25.6 %fusion.16 = bf16[32,2,8,128,128]{4,3,0,2,1:T(8,128)(2,1)} fusion(f32[2,8,32,128,128]{4,3,2,1,0:T(8,128)} %fusion.10, bf16[32,2,8,128,128]{3,4,1,0,2:T(8,128)(2,1)} %fusion.1, bf16[2,8,2,128,128]{4,3,2,1,0:T(8,128)(2,1)S(1)} %copy-done), kind=kOutput, calls=%fused_computation.23 | convolution fusion | flops 2164260864 | bytes 67633152 | tf_op jit(solution)/shard_map/jstac,stcd->jstad/dot_general | solution.py:15
  363.6 23.6 %fusion.19 = bf16[32,2,8,128,128]{4,3,0,2,1:T(8,128)(2,1)} fusion(f32[2,8,32,128,128]{4,3,2,1,0:T(8,128)} %fusion.8, bf16[32,2,8,128,128]{3,4,1,0,2:T(8,128)(2,1)} %fusion.1, bf16[2,8,2,128,128]{4,3,2,1,0:T(8,128)(2,1)S(1)} %copy-done), kind=kOutput, calls=%fused_computation.24 | convolution fusion | flops 2164260864 | bytes 67633152 | tf_op jit(solution)/shard_map/jstac,stcd->jstad/dot_general | solution.py:15
  387.2 0.0 all-gather.2.cloned.1.call-done
  387.2 39.7 %fusion.31 = f32[2,256,32,8]{1,2,3,0:T(8,128)S(1)} fusion(bf16[32,2,8,128,128]{4,3,0,2,1:T(8,128)(2,1)} %fusion.16, bf16[256,2,2,128,128]{4,0,3,1,2:T(8,128)(2,1)} %all-gather.2.cloned.1.call-done), kind=kOutput, calls=%fused_computation.36 | convolution fusion | flops 4294967296 | bytes 34078720 | tf_op jit(solution)/shard_map/jstad,ksad->jstk/dot_general | solution.py:31
  426.9 39.5 %fusion.28 = f32[2,256,32,8]{1,2,3,0:T(8,128)S(1)} fusion(bf16[32,2,8,128,128]{4,3,0,2,1:T(8,128)(2,1)} %fusion.19, bf16[256,2,2,128,128]{4,0,3,1,2:T(8,128)(2,1)} %all-gather.2.cloned.1.call-done), kind=kOutput, calls=%fused_computation.35 | convolution fusion | flops 4294967296 | bytes 34078720 | tf_op jit(solution)/shard_map/jstad,ksad->jstk/dot_general | solution.py:31
  466.4 39.5 %fusion.43 = f32[32,2,8,1,256]{4,0,2,1,3:T(8,128)S(1)} fusion(f32[2,256,32,8]{1,2,3,0:T(8,128)S(1)} %fusion.31, bf16[32,2,8,128,128]{4,3,0,2,1:T(8,128)(2,1)} %fusion.19, bf16[256,2,2,128,128]{4,0,3,1,2:T(8,128)(2,1)} %all-gather.2.cloned.1.call-done), kind=kOutput, calls=%fused_computation.40 | convolution fusion | flops 4295098368 | bytes 34603008 | tf_op jit(solution)/shard_map/jstad,ksad->jstk/dot_general | solution.py:31
  506.0 0.0 copy-start.3
  506.0 32.0 %fusion.49 = f32[32,2,8,1,256]{4,0,2,1,3:T(8,128)S(1)} fusion(f32[2,256,32,8]{1,2,3,0:T(8,128)S(1)} %fusion.28, bf16[32,2,8,128,128]{4,3,0,2,1:T(8,128)(2,1)} %fusion.16, bf16[256,2,2,128,128]{4,0,3,1,2:T(8,128)(2,1)} %all-gather.2.cloned.1.call-done), kind=kOutput, calls=%fused_computation.42 | convolution fusion | flops 4295098368 | bytes 34603008 | tf_op jit(solution)/shard_map/jstad,ksad->jstk/dot_general | solution.py:31
  538.0 0.1 maximum_multiply_fusion
  538.1 2.7 copy.39
  540.8 5.4 gather_fusion
  546.2 0.0 copy-done.3
  546.2 4.0 select_bitcast_fusion
  550.2 4.8 copy.40
  (1 shorter events, 0.0 us)
Async XLA Ops:
  6.5 171.8 %all-reduce.3.cloned.1.call-start = ((), (), s32[]{:S(2)}) async-start(), calls=%async_computation.1 | async-start | bytes 8388608 | tf_op jit(solution)/shard_map/psum | solution.py:9
  20.4 366.8 %all-gather.2.cloned.1.call-start = ((), (), s32[]{:S(2)}) async-start(), calls=%async_computation | async-start | bytes 37748736 | tf_op jit(solution)/shard_map/all_gather | solution.py:56
  196.7 24.1 %copy-start.2 = (s32[256]{0:T(256)S(1)}, s32[256]{0:T(256)}, u32[]{:S(2)}) copy-start(s32[256]{0:T(256)} %param.9) | copy-start | bytes 3076
  196.7 25.2 %copy-start.1 = (bf16[2,8,2,128,128]{4,3,2,1,0:T(8,128)(2,1)S(1)}, bf16[2,8,2,128,128]{4,3,2,1,0:T(8,128)(2,1)}, u32[]{:S(2)}) copy-start(bf16[2,8,2,128,128]{4,3,2,1,0:T(8,128)(2,1)} %param.6) | copy-start | bytes 3145732
  282.4 21.5 %copy-start = (bf16[2,8,2,128,128]{4,3,2,1,0:T(8,128)(2,1)S(1)}, bf16[2,8,2,128,128]{4,3,2,1,0:T(8,128)(2,1)}, u32[]{:S(2)}) copy-start(bf16[2,8,2,128,128]{4,3,2,1,0:T(8,128)(2,1)} %param.7) | copy-start | bytes 3145732
  506.0 40.2 %copy-start.3 = (pred[256]{0:T(512)(128)(4,1)S(1)}, pred[256]{0:T(512)(128)(4,1)}, u32[]{:S(2)}) copy-start(pred[256]{0:T(512)(128)(4,1)} %compare_and_fusion) | copy-start | bytes 772
Sparse Core Ops, SparseCore 0:
  20.6 157.7 all-reduce.2
  183.0 166.2 all-gather.1
where the time goes:
time: 567 us; the launch traced here: 562 us
  matrix products  316 us (56%)
  waiting for transfers between devices  158 us (28%)
  local copies, waits for them, and re-layouts  55 us (10%)
  between operations  18.9 us (3%)
  other arithmetic  14.4 us (3%)
    dot_general x8, matrix products, inner(): return jnp.einsum(spec, first, second, preferred_element_type=jnp.float32)  165 us
    psum x1, waiting for transfers between devices, from_root(): return lax.psum(kept, axis)  158 us
    dot_general x4, matrix products, inner(): jnp.einsum('jstad,ksad->jstk', first, second, preferred_element_type=jnp....  151 us
    unnamed x10, local copies, waits for them, and re-layouts  24.1 us
    slice x1, local copies, waits for them, and re-layouts, body(): phi[:, :, 1]  13.8 us
  transfers between devices with their start and end apart: 2, of which 1 were waited for; matrix products, arithmetic and copies ran while one was open for 36% of the time, Pallas kernels for 0%

commit v1 on v0

v1 whole, which is shorter than its diff:
```python
import functools

import jax
import jax.numpy as jnp
from jax import lax
from jax.experimental import pallas as pl
from jax.experimental.pallas import tpu as pltpu
from jax.sharding import PartitionSpec as P

VMEM_LIMIT = 60 * 1024 * 1024


def sink_kernel(group, left_ref, phi_ref, right_ref, out_ref, wide):
    count = phi_ref.shape[0]
    width = phi_ref.shape[-1]
    for source in range(out_ref.shape[0]):
        left = left_ref[0, source]
        right = right_ref[0, source]

        @pl.loop(0, count // group)
        def _(step):
            start = step * group
            fields = [phi_ref[start + n, 0].reshape(2 * width, width) for n in range(group)]
            mid = jnp.dot(left, jnp.concatenate(fields, 1), preferred_element_type=jnp.float32)
            mid = mid.astype(jnp.bfloat16)
            rows = []
            for n in range(group):
                part = mid[:, n * width:(n + 1) * width]
                rows.append(jnp.concatenate([part[:width], part[width:]], 1))
            sink = jnp.dot(jnp.concatenate(rows, 0), right, preferred_element_type=jnp.float32)
            for n in range(group):
                base = pl.multiple_of((start + n) * width, width)
                for c in range(2):
                    wide[c, pl.ds(base, width), :] = sink[n * width:(n + 1) * width, c * width:(c + 1) * width]

        for c in range(2):

            @pl.loop(0, width, unroll=8)
            def _(row):
                picked = wide[c, pl.ds(row, count, stride=width), :]
                out_ref[source, c, 0, row] = picked.astype(jnp.bfloat16)


def sink_panels(left, phi, right):
    count, times, _, width, _ = phi.shape
    sources = left.shape[1]
    group = 4 if count % 4 == 0 else 1
    mults = 16 * count * times * sources * width ** 3
    return pl.pallas_call(
        functools.partial(sink_kernel, group),
        grid=(times,),
        in_specs=[
            pl.BlockSpec((1, sources, 2 * width, 2 * width), lambda t: (t, 0, 0, 0)),
            pl.BlockSpec((count, 1, 2, width, width), lambda t: (0, t, 0, 0, 0)),
            pl.BlockSpec((1, sources, 2 * width, 2 * width), lambda t: (t, 0, 0, 0)),
        ],
        out_specs=pl.BlockSpec((sources, 2, 1, width, count, width), lambda t: (0, 0, t, 0, 0, 0)),
        out_shape=jax.ShapeDtypeStruct((sources, 2, times, width, count, width), jnp.bfloat16),
        scratch_shapes=[pltpu.VMEM((2, count * width, width), jnp.float32)],
        compiler_params=pltpu.CompilerParams(vmem_limit_bytes=VMEM_LIMIT),
        cost_estimate=pl.CostEstimate(flops=2 * mults, bytes_accessed=6 * phi.size, transcendentals=0),
        name="sink_panels",
    )(left, phi, right)


def corr_kernel(panel_ref, source_ref, partner_ref, out_ref, total):
    step = pl.program_id(0)
    rows, width = panel_ref.shape[3], panel_ref.shape[5]
    half = out_ref.shape[1]
    wide = out_ref.shape[2]

    @pl.when(step == 0)
    def _():
        total[...] = jnp.zeros_like(total)

    panel = jnp.concatenate([panel_ref[0, :, :, r].reshape(2 * half, width) for r in range(rows)], 1)
    for c in range(2):
        source = jnp.concatenate([source_ref[:, 0, c, r].reshape(wide, width) for r in range(rows)], 1)
        total[c] += lax.dot_general(panel, source, (((1,), (1,)), ((), ())), preferred_element_type=jnp.float32)

    @pl.when(step == pl.num_programs(0) - 1)
    def _():
        place = lax.broadcasted_iota(jnp.int32, (wide, wide), 0)
        chosen = jnp.where(place == partner_ref[...], 1.0, 0.0).astype(jnp.float32)

        def permuted(value):
            return jnp.dot(value / width, chosen, precision=lax.Precision.HIGHEST, preferred_element_type=jnp.float32)

        out_ref[0] = permuted(total[0, :half] + total[1, half:])
        out_ref[1] = permuted(total[0, half:] - total[1, :half])


def correlate(panels, which, gathered, partner):
    _, _, times, width, count, _ = panels.shape
    ops, slabs, _, depth, local, _ = gathered.shape
    rows = 8
    per = depth // rows
    wide = ops * local
    flops = 2 * 4 * times * count * wide * width * width
    return pl.pallas_call(
        corr_kernel,
        grid=(slabs * per,),
        in_specs=[
            pl.BlockSpec((1, 2, times, rows, count, width), lambda g: (which, 0, 0, g, 0, 0)),
            pl.BlockSpec((ops, 1, 2, rows, local, width), lambda g: (0, g // per, 0, g % per, 0, 0)),
            pl.BlockSpec((1, wide), lambda g: (0, 0)),
        ],
        out_specs=pl.BlockSpec((2, times * count, wide), lambda g: (0, 0, 0)),
        out_shape=jax.ShapeDtypeStruct((2, times * count, wide), jnp.float32),
        scratch_shapes=[pltpu.VMEM((2, 2 * times * count, wide), jnp.float32)],
        compiler_params=pltpu.CompilerParams(vmem_limit_bytes=VMEM_LIMIT),
        cost_estimate=pl.CostEstimate(flops=flops, bytes_accessed=2 * panels.size, transcendentals=0),
        name="correlate",
    )(panels, gathered, partner)


def body(op, tm, phi, tau_fwd, tau_bwd, src_times, partner):
    count, times, _, width, _ = phi.shape
    sources = tau_fwd.shape[0]
    gathered = []
    for s in range(sources):
        when = src_times[s]
        local = lax.dynamic_index_in_dim(phi, when % times, 1, False)
        local = jnp.where(lax.axis_index("tm") == when // times, local, 0).astype(phi.dtype)
        piece = lax.psum_scatter(local, "tm", scatter_dimension=2, tiled=True)
        piece = jnp.transpose(piece, (1, 2, 0, 3))
        piece = lax.all_gather(piece, ("op", "tm"), axis=0, tiled=False)
        gathered.append(piece.reshape((op, tm) + piece.shape[1:]))

    f_re, f_im = tau_fwd[:, :, 0], tau_fwd[:, :, 1]
    b_re, b_im = tau_bwd[:, :, 0], tau_bwd[:, :, 1]
    left = jnp.concatenate([jnp.concatenate([f_re, -f_im], 3), jnp.concatenate([f_im, f_re], 3)], 2)
    right = jnp.concatenate([jnp.concatenate([b_re, b_im], 3), jnp.concatenate([-b_im, b_re], 3)], 2)
    panels = sink_panels(jnp.swapaxes(left, 0, 1), phi, jnp.swapaxes(right, 0, 1))

    parts = [correlate(panels, s, gathered[s], partner[None, :]) for s in range(sources)]
    corr = jnp.stack(parts, 0).reshape(sources, 2, times, count, -1)
    return jnp.transpose(corr, (3, 0, 2, 1, 4))


def solution(mesh):
    in_specs = (
        P("op", "tm", None, None, None),
        P(None, "tm", None, None, None),
        P(None, "tm", None, None, None),
        P(),
        P(),
    )
    out_specs = P("op", None, "tm", None, None)
    run = functools.partial(body, mesh.shape["op"], mesh.shape["tm"])
    return jax.shard_map(run, mesh=mesh, in_specs=in_specs, out_specs=out_specs, check_vma=False)
```

time: 567 us -> 397 us (0.70)
  matrix products: 316 us -> 0 us
  Pallas kernels: 0 us -> 145 us
  waiting for transfers between devices: 158 us -> 181 us
  local copies, waits for them, and re-layouts: 55 us -> 41.7 us
    dot_general x12 -> x0, matrix products: 316 us -> none  [the longest x8 165 us: inner(): return jnp.einsum(spec, first, second, preferred_element_type=jnp.float32)]
    psum x1 -> x0, waiting for transfers between devices: 158 us -> none  [from_root(): return lax.psum(kept, axis)]
    pallas_call x0 -> x3, Pallas kernels: none -> 145 us  [the longest x1 101 us: sink_panels(): pl.pallas_call(functools.partial(sink_kernel, group), grid=(times,), in_s...]
    reduce_scatter x0 -> x2, waiting for transfers between devices: none -> 90.8 us  [body(): piece = lax.psum_scatter(local, 'tm', scatter_dimension=2, tiled=True)]
    all_gather x1 -> x2, waiting for transfers between devices: 0.01 us -> 89.8 us  [body(): piece = lax.all_gather(piece, ('op', 'tm'), axis=0, tiled=False)]
    all_gather x0 -> x2, local copies, waits for them, and re-layouts: none -> 37.2 us  [body(): piece = lax.all_gather(piece, ('op', 'tm'), axis=0, tiled=False)]
    unnamed x10 -> x4, local copies, waits for them, and re-layouts: 24.1 us -> 0.01 us
    slice x3, local copies, waits for them, and re-layouts: 15.3 us -> 1.52 us  [the longest x1 1.35 us: body(): when = src_times[s]]
  transfers between devices with their start and end apart: 2 -> 4, of which waited for: 1 -> 4; matrix products, arithmetic and copies ran while one was open for 36% -> 6% of each run, Pallas kernels for 0% -> 31%
where the time goes in v1:
time: 397 us; the launch traced here: 396 us
  waiting for transfers between devices  181 us (46%)
  Pallas kernels  145 us (37%)
  local copies, waits for them, and re-layouts  41.7 us (11%)
  between operations  18.4 us (5%)
  other arithmetic  9.53 us (2%)
    pallas_call x1, Pallas kernels, sink_panels(): pl.pallas_call(functools.partial(sink_kernel, group), grid=(times,), in_s...  101 us
    reduce_scatter x2, waiting for transfers between devices, body(): piece = lax.psum_scatter(local, 'tm', scatter_dimension=2, tiled=True)  90.8 us
    all_gather x2, waiting for transfers between devices, body(): piece = lax.all_gather(piece, ('op', 'tm'), axis=0, tiled=False)  89.8 us
    pallas_call x2, Pallas kernels, correlate(): pl.pallas_call(corr_kernel, grid=(slabs * per,), in_specs=[pl.BlockSpec((...  43.6 us
    all_gather x2, local copies, waits for them, and re-layouts, body(): piece = lax.all_gather(piece, ('op', 'tm'), axis=0, tiled=False)  37.2 us
  transfers between devices with their start and end apart: 4, of which 4 were waited for; matrix products, arithmetic and copies ran while one was open for 6% of the time, Pallas kernels for 31%

profile of v1, /device:TPU:0, one launch (start us, length us, event | category | flops | bytes accessed | tf_op | source)
XLA Modules:
  0.0 395.6 jit_solution(5408718808868429792)
XLA Ops:
  6.5 0.0 reduce-scatter.3.cloned.1.call-start
  6.5 1.3 fusion.4
  13.0 4.5 %select_bitcast_fusion.1 = (bf16[32,2,128,128]{3,2,1,0:T(8,128)(2,1)}, bf16[32,2,128,128]{3,2,1,0:T(8,128)(2,1)}) fusion(bf16[32,8,2,128,128]{4,3,2,1,0:T(8,128)(2,1)} %phi_ref.1, s32[]{:T(128)S(6)} %select_n.48, pred[]{:T(512)S(6)} %eq.9, s32[]{:T(128)S(6)} %select_n.54, pred[]{:T(512)S(6)} %eq.10), kind=kLoop, calls=%fused_computation.3 | loop fusion | flops 2097152 | bytes 8388618 | tf_op jit(solution)/shard_map/jit(_where)/select_n | solution.py:124
  17.5 0.0 copy-start
  17.5 0.0 reduce-scatter.3.cloned.1.call-update
  17.5 0.0 reduce-scatter.5.cloned.1.call-start
  17.6 0.7 reduce-scatter.5.cloned.1.call-update
  18.3 0.0 all-gather.5.cloned.1.call-start
  18.3 45.7 %reduce-scatter.3.cloned.1.call-done = bf16[32,2,32,128]{3,2,1,0:T(8,128)(2,1)} async-done(((bf16[32,2,128,128]{3,2,1,0:T(8,128)(2,1)}), bf16[32,2,32,128]{3,2,1,0:T(8,128)(2,1)}) %reduce-scatter.3.cloned.1.call-update) | async-done | bytes 524304 | tf_op jit(solution)/shard_map/reduce_scatter | solution.py:125
  64.1 0.0 all-gather.5.cloned.1.call-update
  64.1 0.0 all-gather.7.cloned.1.call-start
  64.1 45.1 %reduce-scatter.5.cloned.1.call-done = bf16[32,2,32,128]{3,2,1,0:T(8,128)(2,1)} async-done(((bf16[32,2,128,128]{3,2,1,0:T(8,128)(2,1)}), bf16[32,2,32,128]{3,2,1,0:T(8,128)(2,1)}) %reduce-scatter.5.cloned.1.call-update) | async-done | bytes 524304 | tf_op jit(solution)/shard_map/reduce_scatter | solution.py:125
  109.2 0.0 all-gather.7.cloned.1.call-update
  109.3 0.0 copy-done
  109.3 0.0 copy-start.1
  109.3 0.1 fusion.2
  109.4 0.1 fusion.1
  109.5 0.1 copy_bitcast_fusion
  109.5 1.7 maximum_bitcast_fusion.1.right_ref
  111.2 0.0 copy-done.1
  111.2 0.1 fusion.3
  111.3 0.1 fusion
  111.4 0.1 copy_bitcast_fusion.2
  111.4 1.6 maximum_bitcast_fusion.left_ref
  113.1 100.9 %sink_panels.1.panel_ref = bf16[2,2,8,128,32,128]{5,4,3,2,1,0:T(8,128)(2,1)} custom-call(bf16[8,2,256,256]{3,2,1,0:T(8,128)(2,1)} %maximum_bitcast_fusion.left_ref, bf16[32,8,2,128,128]{4,3,2,1,0:T(8,128)(2,1)} %phi_ref.1, bf16[8,2,256,256]{3,2,1,0:T(8,128)(2,1)} %maximum_bitcast_fusion.1.right_ref), custom_call_target="tpu_custom_call" | custom-call | flops 34359738368 | bytes 50331648 | tf_op jit(solution)/shard_map/sink_panels/pallas_call | solution.py:49
  214.0 13.7 %all-gather.5.cloned.1.call-done = bf16[64,32,32,128]{3,1,0,2:T(8,128)(2,1)} async-done(((bf16[2,32,32,128]{3,1,0,2:T(8,128)(2,1)}), bf16[64,32,32,128]{3,1,0,2:T(8,128)(2,1)}) %all-gather.5.cloned.1.call-update) | async-done | bytes 16777232 | tf_op jit(solution)/shard_map/all_gather | solution.py:127
  227.7 18.6 %copy.10 = bf16[64,32,32,128]{3,2,1,0:T(8,128)(2,1)} copy(bf16[64,32,32,128]{3,1,0,2:T(8,128)(2,1)} %all-gather.5.cloned.1.call-done) | data formatting | bytes 33554432 | tf_op jit(solution)/shard_map/all_gather | solution.py:127
  246.4 21.9 %correlate.2 = f32[2,256,256]{2,1,0:T(8,128)} custom-call(bf16[2,2,8,128,32,128]{5,4,3,2,1,0:T(8,128)(2,1)} %sink_panels.1.panel_ref, bf16[8,4,2,32,32,128]{5,4,3,2,1,0:T(8,128)(2,1)} %bitcast.32, s32[1,256]{1,0:T(1,128)} %bitcast.37), custom_call_target="tpu_custom_call" | custom-call | flops 8589934592 | bytes 33554432 | tf_op jit(solution)/shard_map/correlate/pallas_call | solution.py:100
  268.2 1.4 copy.12
  269.7 76.1 %all-gather.7.cloned.1.call-done = bf16[64,32,32,128]{3,1,0,2:T(8,128)(2,1)} async-done(((bf16[2,32,32,128]{3,1,0,2:T(8,128)(2,1)}), bf16[64,32,32,128]{3,1,0,2:T(8,128)(2,1)}) %all-gather.7.cloned.1.call-update) | async-done | bytes 16777232 | tf_op jit(solution)/shard_map/all_gather | solution.py:127
  345.8 18.6 %copy.11 = bf16[64,32,32,128]{3,2,1,0:T(8,128)(2,1)} copy(bf16[64,32,32,128]{3,1,0,2:T(8,128)(2,1)} %all-gather.7.cloned.1.call-done) | data formatting | bytes 33554432 | tf_op jit(solution)/shard_map/all_gather | solution.py:127
  364.3 21.7 %correlate.3 = f32[2,256,256]{2,1,0:T(8,128)} custom-call(bf16[2,2,8,128,32,128]{5,4,3,2,1,0:T(8,128)(2,1)} %sink_panels.1.panel_ref, bf16[8,4,2,32,32,128]{5,4,3,2,1,0:T(8,128)(2,1)} %bitcast.31, s32[1,256]{1,0:T(1,128)} %bitcast.38), custom_call_target="tpu_custom_call" | custom-call | flops 8589934592 | bytes 33554432 | tf_op jit(solution)/shard_map/correlate/pallas_call | solution.py:100
  386.1 1.4 copy.13
  387.5 1.6 maximum_bitcast_fusion.2
Async XLA Ops:
  6.5 57.5 %reduce-scatter.3.cloned.1.call-start = ((), (), s32[]{:S(2)}) async-start(), calls=%async_computation.2 | async-start | bytes 2621440 | tf_op jit(solution)/shard_map/reduce_scatter | solution.py:125
  17.5 91.7 %copy-start = (bf16[2,8,2,128,128]{4,3,2,1,0:T(8,128)(2,1)S(1)}, bf16[2,8,2,128,128]{4,3,2,1,0:T(8,128)(2,1)}, u32[]{:S(2)}) copy-start(bf16[2,8,2,128,128]{4,3,2,1,0:T(8,128)(2,1)} %param.7) | copy-start | bytes 3145732
  17.5 91.7 %reduce-scatter.5.cloned.1.call-start = ((), (), s32[]{:S(2)}) async-start(), calls=%async_computation.3 | async-start | bytes 2621440 | tf_op jit(solution)/shard_map/reduce_scatter | solution.py:125
  18.3 209.4 %all-gather.5.cloned.1.call-start = ((), (), s32[]{:S(2)}) async-start(), calls=%async_computation.4 | async-start | bytes 17301504 | tf_op jit(solution)/shard_map/all_gather | solution.py:127
  64.1 281.7 %all-gather.7.cloned.1.call-start = ((), (), s32[]{:S(2)}) async-start(), calls=%async_computation.5 | async-start | bytes 17301504 | tf_op jit(solution)/shard_map/all_gather | solution.py:127
  109.3 1.9 copy-start.1
Sparse Core Ops, SparseCore 0:
  17.7 46.3 reduce-scatter.2
  66.3 42.8 reduce-scatter.4
  112.2 115.4 all-gather.4
  230.6 115.1 all-gather.6
